TPU v7x, 32 devices: a whole 2x2x4 slice. The times are simulated.
32 devices in a mesh: scen: 8 (over z, x), row: 2 (over core), col: 2 (over y).
Axes of the slice: x: 2, y: 2, z: 4, core: 2. Of those that a mesh axis runs over, the one named last changes fastest.
Arguments:
- kkt: float32 [24, 768, 768], P('scen', ('row', 'col')), as said below
- border: float32 [24, 768, 4096], P('scen', None, ('row', 'col')), may hold values from -0.21875 to 0.21875
- first_diag: float32 [4096], P('scen'), may hold values from 0.5 to 1.5
- assignment: int32 [24], P('scen'), may hold values from 0 to 23, as said below
- panel: int32 [8], replicated, may hold values from 0 to 7, each once
Outputs:
- schur: float32 [4096, 4096], P('scen', ('row', 'col'))
- panel_factor: float32 [4096, 512], P('scen', ('row', 'col'))
Inputs may be any that keep to these rules, and one draw needn't show every extreme that they name: assignment is a permutation; with k = d * 3 + j (0 <= j < 3), assignment[k] is either k or (d XOR 1) * 3 + j, and the two scenarios of such a pair are either both fixed or swapped. panel is a permutation. Each kkt block is symmetric positive definite; after scaling by its diagonal, the off-diagonal part has spectral norm about one half.
All inputs are finite; a program needn't handle non-finite values.
Results may differ from a plain program's by a relative error of at most 0.00015.
Values sent between devices are 32-bit elements; how exact they have to be, the bound alone decides.
A program may use at most 192 MiB of HBM per device.

v0:
```python
import jax
import jax.numpy as jnp
from jax import lax
from jax.sharding import PartitionSpec as P

NK = 768
NF = 4096
PW = 512
NEWTON = 3
HIGH = lax.Precision.HIGHEST


def swapped(value, axis, distance):
    mask = 2**distance
    pairs = [(source, source ^ mask) for source in range(lax.axis_size(axis))]
    return lax.ppermute(value, axis, pairs)


def matmul(left, right):
    return jnp.dot(left, right, precision=HIGH, preferred_element_type=jnp.float32)


def contract(left, right):
    return lax.dot_general(
        left, right, (((0,), (0,)), ((), ())), precision=HIGH, preferred_element_type=jnp.float32
    )


def body(kkt, border, first_diag, assignment, panel):
    scen_index = lax.axis_index("scen")
    own_index = lax.axis_index(("row", "col"))
    slots = kkt.shape[0]
    partner = swapped(border, "scen", 0)
    kkt_all = lax.all_gather(kkt, ("row", "col"), axis=1, tiled=True)
    row_count = kkt.shape[1]
    col_count = border.shape[2]
    first_row = own_index * row_count
    row_ids = first_row + jnp.arange(row_count, dtype=jnp.int32)
    eye_rows = (jnp.arange(NK, dtype=jnp.int32)[None, :] == row_ids[:, None]).astype(jnp.float32)
    tile_total = jnp.zeros((NF, col_count), jnp.float32)
    for slot in range(slots):
        scenario_id = scen_index * slots + slot
        chosen = jnp.where(assignment[slot] == scenario_id, border[slot], partner[slot])
        kkt_rows = kkt[slot]
        kkt_full = kkt_all[slot]
        inv_diag = 1.0 / jnp.diagonal(kkt_full)
        local_inv = lax.dynamic_slice_in_dim(inv_diag, first_row, row_count)
        approx = (
            2.0 * (eye_rows * local_inv[:, None])
            - local_inv[:, None] * kkt_rows * inv_diag[None, :]
        )
        for step in range(NEWTON - 1):
            left = matmul(approx, kkt_full)

            def add_block(total, piece, start, left=left):
                return matmul(left, piece)

            product = add_block(
                jnp.zeros_like(approx),
                lax.all_gather(approx, ("row", "col"), axis=0, tiled=True),
                jnp.int32(0),
            )
            approx = 2.0 * approx - product

        def solve_piece(piece, start, chosen=chosen):
            return matmul(piece, chosen)

        solved = solve_piece(
            lax.all_gather(approx, ("row", "col"), axis=0, tiled=True), jnp.int32(0)
        )

        def border_piece(piece, start, solved=solved):
            return contract(piece, solved)

        tile = border_piece(
            lax.all_gather(chosen, ("row", "col"), axis=1, tiled=True), jnp.int32(0)
        )
        tile_total = tile_total + tile
    summed = lax.psum_scatter(tile_total, "scen", scatter_dimension=0, tiled=True)
    row_span = summed.shape[0]
    global_rows = scen_index * row_span + jnp.arange(row_span, dtype=jnp.int32)
    global_cols = own_index * col_count + jnp.arange(col_count, dtype=jnp.int32)
    on_diag = global_rows[:, None] == global_cols[None, :]
    schur = summed + jnp.where(on_diag, first_diag[:, None], 0.0)
    panel_start = panel[0] * PW
    panel_ids = panel_start + jnp.arange(PW, dtype=jnp.int32)
    select_cols = (global_cols[:, None] == panel_ids[None, :]).astype(jnp.float32)
    select_rows = (panel_ids[:, None] == global_rows[None, :]).astype(jnp.float32)
    panel_rows = lax.psum(matmul(schur, select_cols), ("row", "col"))
    block = lax.psum(matmul(select_rows, panel_rows), "scen")
    symmetric = 0.5 * (block + block.T)
    lower_factor = jnp.linalg.cholesky(symmetric)
    factor = lax.linalg.triangular_solve(
        lower_factor, panel_rows, left_side=False, lower=True, transpose_a=True
    )
    share = PW // lax.axis_size(("row", "col"))
    own_cols = lax.dynamic_slice_in_dim(factor, own_index * share, share, 1)
    return (schur, own_cols)


def solution(mesh):
    in_specs = (
        P("scen", ("row", "col"), None),
        P("scen", None, ("row", "col")),
        P("scen"),
        P("scen"),
        P(),
    )
    out_specs = (P("scen", ("row", "col")), P("scen", ("row", "col")))
    return jax.shard_map(body, mesh=mesh, in_specs=in_specs, out_specs=out_specs, check_vma=False)
```

profile of v0, /device:TPU:0, one launch (start us, length us, event | category | flops | bytes accessed | tf_op | source)
XLA Modules:
  0.0 1276.0 jit_solution(8011691956616219220)
XLA Ops:
  8.0 55.1 %all-gather.17.cloned.1.call-done = f32[3,768,768]{2,1,0:T(8,128)} async-done(((f32[3,192,768]{2,1,0:T(8,128)}), f32[3,768,768]{2,1,0:T(8,128)}) %all-gather.17.cloned.1.call-update) | async-done | bytes 7077904 | tf_op jit(solution)/shard_map/all_gather | solution.py:34
  63.1 5.7 slice_bitcast_fusion
  68.8 12.2 gather_fusion.1
  81.0 12.1 gather_fusion.2
  93.3 6.3 gather_fusion
  99.7 3.1 fusion.30
  104.1 3.5 fusion.27
  107.7 19.3 %all-gather.31.cloned.1.call-done = f32[768,768]{1,0:T(8,128)} async-done(((f32[192,768]{1,0:T(8,128)}), f32[768,768]{1,0:T(8,128)}) %all-gather.31.cloned.1.call-update) | async-done | bytes 2359312 | tf_op jit(solution)/shard_map/all_gather | solution.py:60
  127.0 4.3 convolution_subtract_fusion.1
  131.3 3.6 fusion.31
  134.9 17.8 %all-gather.25.cloned.1.call-done = f32[768,768]{1,0:T(8,128)} async-done(((f32[192,768]{1,0:T(8,128)}), f32[768,768]{1,0:T(8,128)}) %all-gather.25.cloned.1.call-update) | async-done | bytes 2359312 | tf_op jit(solution)/shard_map/all_gather | solution.py:60
  152.7 4.2 convolution_subtract_fusion.3
  157.2 3.5 fusion.35
  160.7 17.4 %all-gather.19.cloned.1.call-done = f32[768,768]{1,0:T(8,128)} async-done(((f32[192,768]{1,0:T(8,128)}), f32[768,768]{1,0:T(8,128)}) %all-gather.19.cloned.1.call-update) | async-done | bytes 2359312 | tf_op jit(solution)/shard_map/all_gather | solution.py:60
  178.1 4.2 convolution_subtract_fusion.5
  182.4 3.4 fusion.109
  185.8 17.8 %all-gather.33.cloned.1.call-done = f32[768,768]{1,0:T(8,128)} async-done(((f32[192,768]{1,0:T(8,128)}), f32[768,768]{1,0:T(8,128)}) %all-gather.33.cloned.1.call-update) | async-done | bytes 2359312 | tf_op jit(solution)/shard_map/all_gather | solution.py:60
  203.6 4.2 convolution_subtract_fusion
  209.4 3.4 fusion.108
  212.9 16.2 %all-gather.27.cloned.1.call-done = f32[768,768]{1,0:T(8,128)} async-done(((f32[192,768]{1,0:T(8,128)}), f32[768,768]{1,0:T(8,128)}) %all-gather.27.cloned.1.call-update) | async-done | bytes 2359312 | tf_op jit(solution)/shard_map/all_gather | solution.py:60
  229.1 4.2 convolution_subtract_fusion.2
  233.8 3.4 fusion.107
  237.2 18.1 %all-gather.21.cloned.1.call-done = f32[768,768]{1,0:T(8,128)} async-done(((f32[192,768]{1,0:T(8,128)}), f32[768,768]{1,0:T(8,128)}) %all-gather.21.cloned.1.call-update) | async-done | bytes 2359312 | tf_op jit(solution)/shard_map/all_gather | solution.py:60
  255.3 4.2 convolution_subtract_fusion.4
  262.2 151.2 %collective-permute-done = f32[3,768,1024]{2,1,0:T(8,128)} collective-permute-done((f32[3,768,1024]{2,1,0:T(8,128)}, f32[3,768,1024]{2,1,0:T(8,128)}, u32[]{:S(2)}, u32[]{:S(2)}) %collective-permute-start) | collective-permute-done | bytes 9437216 | tf_op jit(solution)/shard_map/ppermute | solution.py:16
  413.3 11.1 slice_select_fusion
  426.9 10.4 fusion.8
  437.3 12.2 fusion.10
  449.6 10.4 fusion.12
  460.0 46.7 %all-gather.39.cloned.1.call-done = f32[1,768,4096]{2,1,0:T(8,128)} async-done(((f32[1,768,1024]{2,1,0:T(8,128)}), f32[1,768,4096]{2,1,0:T(8,128)}) %all-gather.39.cloned.1.call-update) | async-done | bytes 12582928 | tf_op jit(solution)/shard_map/all_gather | solution.py:76
  506.7 45.4 %fusion.2 = f32[4096,1024]{1,0:T(8,128)} fusion(f32[768,1024]{1,0:T(8,128)} %fusion.10, f32[1,768,4096]{2,1,0:T(8,128)} %all-gather.39.cloned.1.call-done), kind=kOutput, calls=%fused_computation.8 | convolution fusion | flops 38654705664 | bytes 32505856 | tf_op jit(solution)/shard_map/dot_general | solution.py:24
  552.2 38.1 %all-gather.37.cloned.1.call-done = f32[1,768,4096]{2,1,0:T(8,128)} async-done(((f32[1,768,1024]{2,1,0:T(8,128)}), f32[1,768,4096]{2,1,0:T(8,128)}) %all-gather.37.cloned.1.call-update) | async-done | bytes 12582928 | tf_op jit(solution)/shard_map/all_gather | solution.py:76
  590.2 45.5 %fusion.4 = f32[4096,1024]{1,0:T(8,128)} fusion(f32[768,1024]{1,0:T(8,128)} %fusion.12, f32[1,768,4096]{2,1,0:T(8,128)} %all-gather.37.cloned.1.call-done), kind=kOutput, calls=%fused_computation.10 | convolution fusion | flops 38654705664 | bytes 32505856 | tf_op jit(solution)/shard_map/dot_general | solution.py:24
  635.8 38.1 %all-gather.41.cloned.1.call-done = f32[1,768,4096]{2,1,0:T(8,128)} async-done(((f32[1,768,1024]{2,1,0:T(8,128)}), f32[1,768,4096]{2,1,0:T(8,128)}) %all-gather.41.cloned.1.call-update) | async-done | bytes 12582928 | tf_op jit(solution)/shard_map/all_gather | solution.py:76
  673.9 47.5 %add_add_fusion = f32[4096,1024]{1,0:T(8,128)} fusion(f32[4096,1024]{1,0:T(8,128)} %fusion.4, f32[4096,1024]{1,0:T(8,128)} %fusion.2, f32[768,1024]{1,0:T(8,128)S(1)} %copy-done.3, f32[1,768,4096]{2,1,0:T(8,128)} %all-gather.41.cloned.1.call-done), kind=kOutput, calls=%fused_computation.5 | convolution fusion | flops 38663094272 | bytes 66060288 | tf_op jit(solution)/shard_map/dot_general | solution.py:24
  722.2 279.8 %reduce-scatter.2.cloned.1.call-done = f32[512,1024]{1,0:T(8,128)} async-done(((f32[4096,1024]{1,0:T(8,128)}), f32[512,1024]{1,0:T(8,128)}) %reduce-scatter.2.cloned.1.call-update) | async-done | bytes 2097168 | tf_op jit(solution)/shard_map/reduce_scatter | solution.py:79
  1008.4 35.3 %all-reduce.4.cloned.1.call-done = f32[512,512]{1,0:T(8,128)} async-done(((f32[512,512]{1,0:T(8,128)}), f32[512,512]{1,0:T(8,128)}) %all-reduce.4.cloned.1.call-update) | async-done | bytes 1048592 | tf_op jit(solution)/shard_map/psum | solution.py:89
  1043.7 3.4 fusion.20
  1047.1 78.9 %all-reduce.6.cloned.1.call-done = f32[512,512]{0,1:T(8,128)} async-done(((f32[512,512]{0,1:T(8,128)}), f32[512,512]{0,1:T(8,128)}) %all-reduce.6.cloned.1.call-update) | async-done | bytes 1048592 | tf_op jit(solution)/shard_map/psum | solution.py:90
  1128.5 11.7 cholesky.104
  1140.4 9.8 custom-call.30
  1150.9 11.9 cholesky.217
  1164.1 9.8 custom-call.31
  1174.6 11.7 cholesky.238
  1187.0 9.8 custom-call.32
  1197.5 11.9 cholesky.255
  1212.7 10.4 while.1
  1223.2 40.1 %custom-call.33 = f32[4,128,128]{1,2,0:T(8,128)S(1)} custom-call(f32[4,128,128]{2,1,0:T(8,128)} %get-tuple-element.9), custom_call_target="InvertDiagBlocksLowerTriangular" | custom-call | tf_op jit(solution)/shard_map/triangular_solve | solution.py:93
  (128 shorter events, 38.5 us)
Async XLA Ops:
  7.2 56.0 %all-gather.17.cloned.1.call-start = ((), (), s32[]{:S(2)}) async-start(), calls=%async_computation.1 | async-start | bytes 8847360 | tf_op jit(solution)/shard_map/all_gather | solution.py:34
  7.9 119.1 %all-gather.31.cloned.1.call-start = ((), (), s32[]{:S(2)}) async-start(), calls=%async_computation.8 | async-start | bytes 2949120 | tf_op jit(solution)/shard_map/all_gather | solution.py:60
  99.6 4.5 copy-start.2
  102.8 49.9 %all-gather.25.cloned.1.call-start = ((), (), s32[]{:S(2)}) async-start(), calls=%async_computation.5 | async-start | bytes 2949120 | tf_op jit(solution)/shard_map/all_gather | solution.py:60
  102.8 24.2 %copy-start.9 = (f32[192,768]{1,0:T(8,128)S(1)}, f32[192,768]{1,0:T(8,128)}, u32[]{:S(2)}) copy-start(f32[192,768]{1,0:T(8,128)} %get-tuple-element.30) | copy-start | bytes 1769476
  103.5 74.6 %all-gather.19.cloned.1.call-start = ((), (), s32[]{:S(2)}) async-start(), calls=%async_computation.2 | async-start | bytes 2949120 | tf_op jit(solution)/shard_map/all_gather | solution.py:60
  104.1 99.5 %all-gather.33.cloned.1.call-start = ((), (), s32[]{:S(2)}) async-start(), calls=%async_computation.9 | async-start | bytes 2949120 | tf_op jit(solution)/shard_map/all_gather | solution.py:60
  131.3 21.4 %copy-start.8 = (f32[192,768]{1,0:T(8,128)S(1)}, f32[192,768]{1,0:T(8,128)}, u32[]{:S(2)}) copy-start(f32[192,768]{1,0:T(8,128)} %get-tuple-element.32) | copy-start | bytes 1769476
  131.3 97.8 %all-gather.27.cloned.1.call-start = ((), (), s32[]{:S(2)}) async-start(), calls=%async_computation.6 | async-start | bytes 2949120 | tf_op jit(solution)/shard_map/all_gather | solution.py:60
  156.9 21.2 %copy-start.7 = (f32[192,768]{1,0:T(8,128)S(1)}, f32[192,768]{1,0:T(8,128)}, u32[]{:S(2)}) copy-start(f32[192,768]{1,0:T(8,128)} %get-tuple-element.31) | copy-start | bytes 1769476
  156.9 98.4 %all-gather.21.cloned.1.call-start = ((), (), s32[]{:S(2)}) async-start(), calls=%async_computation.3 | async-start | bytes 2949120 | tf_op jit(solution)/shard_map/all_gather | solution.py:60
  160.7 21.7 %copy-start.5 = (f32[192,768]{1,0:T(8,128)S(1)}, f32[192,768]{1,0:T(8,128)}, u32[]{:S(2)}) copy-start(f32[192,768]{1,0:T(8,128)} %convolution_subtract_fusion.1) | copy-start | bytes 1769476
  182.4 243.5 %all-gather.35.cloned.1.call-start = ((), (), s32[]{:S(2)}) async-start(), calls=%async_computation.10 | async-start | bytes 2949120 | tf_op jit(solution)/shard_map/all_gather | solution.py:69
  185.8 23.6 %copy-start.4 = (f32[192,768]{1,0:T(8,128)S(1)}, f32[192,768]{1,0:T(8,128)}, u32[]{:S(2)}) copy-start(f32[192,768]{1,0:T(8,128)} %convolution_subtract_fusion.3) | copy-start | bytes 1769476
  207.9 229.5 %all-gather.29.cloned.1.call-start = ((), (), s32[]{:S(2)}) async-start(), calls=%async_computation.7 | async-start | bytes 2949120 | tf_op jit(solution)/shard_map/all_gather | solution.py:69
  207.9 205.4 %collective-permute-start = (f32[3,768,1024]{2,1,0:T(8,128)}, f32[3,768,1024]{2,1,0:T(8,128)}, u32[]{:S(2)}, u32[]{:S(2)}) collective-permute-start(f32[3,768,1024]{2,1,0:T(8,128)} %param.6), channel_id=1, source_target_pairs={{0,4},{4,0},{8,12},{12,8},{16,20},{20,16},{24,28},{28,24},{1,5},{5... | collective-permute-start | bytes 28311560 | tf_op jit(solution)/shard_map/ppermute | solution.py:16
  212.9 20.9 %copy-start.6 = (f32[192,768]{1,0:T(8,128)S(1)}, f32[192,768]{1,0:T(8,128)}, u32[]{:S(2)}) copy-start(f32[192,768]{1,0:T(8,128)} %convolution_subtract_fusion.5) | copy-start | bytes 1769476
  233.3 216.2 %all-gather.23.cloned.1.call-start = ((), (), s32[]{:S(2)}) async-start(), calls=%async_computation.4 | async-start | bytes 2949120 | tf_op jit(solution)/shard_map/all_gather | solution.py:69
  237.2 22.4 %copy-start.13 = (s32[3]{0:T(128)S(1)}, s32[3]{0:T(128)}, u32[]{:S(2)}) copy-start(s32[3]{0:T(128)} %param.8) | copy-start | bytes 40
  259.6 247.2 %all-gather.39.cloned.1.call-start = ((), (), s32[]{:S(2)}) async-start(), calls=%async_computation.15 | async-start | bytes 15728640 | tf_op jit(solution)/shard_map/all_gather | solution.py:76
  424.5 165.8 %all-gather.37.cloned.1.call-start = ((), (), s32[]{:S(2)}) async-start(), calls=%async_computation.14 | async-start | bytes 15728640 | tf_op jit(solution)/shard_map/all_gather | solution.py:76
  425.1 1.9 copy-start
  425.1 248.8 %all-gather.41.cloned.1.call-start = ((), (), s32[]{:S(2)}) async-start(), calls=%async_computation.16 | async-start | bytes 15728640 | tf_op jit(solution)/shard_map/all_gather | solution.py:76
  425.8 576.1 %reduce-scatter.2.cloned.1.call-start = ((), (), s32[]{:S(2)}) async-start(), calls=%async_computation.11 | async-start | bytes 18874368 | tf_op jit(solution)/shard_map/reduce_scatter | solution.py:79
  437.3 12.2 copy-start.1
  552.2 121.8 %copy-start.3 = (f32[768,1024]{1,0:T(8,128)S(1)}, f32[768,1024]{1,0:T(8,128)}, u32[]{:S(2)}) copy-start(f32[768,1024]{1,0:T(8,128)} %fusion.8) | copy-start | bytes 9437188
  721.4 0.7 copy-start.15
  721.4 280.5 %copy-start.14 = (f32[512]{0:T(512)S(1)}, f32[512]{0:T(512)}, u32[]{:S(2)}) copy-start(f32[512]{0:T(512)} %param.7) | copy-start | bytes 6148
  721.5 322.2 %all-reduce.4.cloned.1.call-start = ((), (), s32[]{:S(2)}) async-start(), calls=%async_computation.12 | async-start | bytes 2097152 | tf_op jit(solution)/shard_map/psum | solution.py:89
  1003.8 1.3 copy-start.12
  1008.2 117.9 %all-reduce.6.cloned.1.call-start = ((), (), s32[]{:S(2)}) async-start(), calls=%async_computation.13 | async-start | bytes 2097152 | tf_op jit(solution)/shard_map/psum | solution.py:90
  1126.0 1.7 copy-start.10
  1174.2 89.1 %copy-start.11 = (f32[512,512]{1,0:T(8,128)S(1)}, f32[512,512]{1,0:T(8,128)}, u32[]{:S(2)}) copy-start(f32[512,512]{1,0:T(8,128)} %all-reduce.4.cloned.1.call-done) | copy-start | bytes 3145732
Sparse Core Ops, SparseCore 0:
  9.5 53.5 all-gather.16
  102.9 24.0 all-gather.30
  128.5 24.0 all-gather.24
  154.1 23.9 all-gather.18
  179.5 24.0 all-gather.32
  205.0 24.0 all-gather.26
  231.2 24.0 all-gather.20
  256.9 24.0 all-gather.34
  282.5 24.0 all-gather.28
  308.6 24.0 all-gather.22
  424.6 82.0 all-gather.38
  508.1 82.0 all-gather.36
  591.8 82.0 all-gather.40
  721.6 280.2 reduce-scatter.1
  1008.3 35.3 all-reduce.3
  1047.2 78.7 all-reduce.5
where the time goes:
time: 1290 us; the launch traced here: 1280 us
  waiting for transfers between devices  833 us (65%)
  matrix products  231 us (18%)
  other arithmetic  136 us (11%)
  local copies, waits for them, and re-layouts  53.5 us (4%)
  between operations  19.3 us (1%)
    reduce_scatter x1, waiting for transfers between devices, body(): lax.psum_scatter(tile_total, 'scen', scatter_dimension=0, tiled=True)  280 us
    ppermute x1, waiting for transfers between devices, swapped(): return lax.ppermute(value, axis, pairs)  151 us
    dot_general x3, matrix products, contract(): lax.dot_general(left, right, (((0,), (0,)), ((), ())), precision=HIGH, pr...  138 us
    all_gather x3, waiting for transfers between devices, body(): lax.all_gather(chosen, ('row', 'col'), axis=1, tiled=True)  123 us
    all_gather x9, waiting for transfers between devices, body(): lax.all_gather(approx, ('row', 'col'), axis=0, tiled=True)  107 us
    dot_general x17, matrix products, matmul(): jnp.dot(left, right, precision=HIGH, preferred_element_type=jnp.float32)  85.6 us
    another operation x15, other arithmetic, body(): lower_factor = jnp.linalg.cholesky(symmetric)  79.5 us
    psum x1, waiting for transfers between devices, body(): block = lax.psum(matmul(select_rows, panel_rows), 'scen')  78.9 us
  transfers between devices with their start and end apart: 17, of which 14 were waited for; matrix products, arithmetic and copies ran while one was open for 14% of the time, Pallas kernels for 0%

commit v1 on v0

--- a/solution.py
+++ b/solution.py
@@ -73,7 +73,13 @@
             return contract(piece, solved)
 
         tile = border_piece(
-            lax.all_gather(chosen, ("row", "col"), axis=1, tiled=True), jnp.int32(0)
+            jnp.concatenate(
+                lax.all_to_all(
+                    jnp.stack([chosen] * lax.axis_size(("row", "col"))), ("row", "col"), 0, 0
+                ),
+                axis=1,
+            ),
+            jnp.int32(0),
         )
         tile_total = tile_total + tile
     summed = lax.psum_scatter(tile_total, "scen", scatter_dimension=0, tiled=True)

time: 1290 us -> 1370 us (1.062)
  local copies, waits for them, and re-layouts: 53.5 us -> 84.3 us
  waiting for transfers between devices: 833 us -> 863 us
  starting transfers between devices: 2.97 us -> 23.8 us
    all_to_all x0 -> x3, waiting for transfers between devices: none -> 290 us  [body(): lax.all_to_all(jnp.stack([chosen] * lax.axis_size(('row', 'col'))), ('row...]
    all_gather x3 -> x0, waiting for transfers between devices: 123 us -> none  [body(): lax.all_gather(chosen, ('row', 'col'), axis=1, tiled=True)]
    all_gather x9, waiting for transfers between devices: 107 us -> 16.5 us  [body(): lax.all_gather(approx, ('row', 'col'), axis=0, tiled=True)]
    ppermute x1, waiting for transfers between devices: 151 us -> 108 us  [swapped(): return lax.ppermute(value, axis, pairs)]
    another operation x12 -> x18, local copies, waits for them, and re-layouts: 10.4 us -> 42.2 us  [the longest x6 31.7 us: body(): jnp.stack([chosen] * lax.axis_size(('row', 'col')))]
    all_to_all x0 -> x3, starting transfers between devices: none -> 19 us  [body(): lax.all_to_all(jnp.stack([chosen] * lax.axis_size(('row', 'col'))), ('row...]
  transfers between devices with their start and end apart: 17 -> 17, of which waited for: 14 -> 9; matrix products, arithmetic and copies ran while one was open for 14% -> 19% of each run, Pallas kernels for 0% -> 0%
where the time goes in v1:
time: 1370 us; the launch traced here: 1360 us
  waiting for transfers between devices  863 us (63%)
  matrix products  236 us (17%)
  other arithmetic  137 us (10%)
  local copies, waits for them, and re-layouts  84.3 us (6%)
  starting transfers between devices  23.8 us (2%)
  between operations  18.9 us (1%)
    all_to_all x3, waiting for transfers between devices, body(): lax.all_to_all(jnp.stack([chosen] * lax.axis_size(('row', 'col'))), ('row...  290 us
    reduce_scatter x1, waiting for transfers between devices, body(): lax.psum_scatter(tile_total, 'scen', scatter_dimension=0, tiled=True)  280 us
    dot_general x3, matrix products, contract(): lax.dot_general(left, right, (((0,), (0,)), ((), ())), precision=HIGH, pr...  137 us
    ppermute x1, waiting for transfers between devices, swapped(): return lax.ppermute(value, axis, pairs)  108 us
    dot_general x17, matrix products, matmul(): jnp.dot(left, right, precision=HIGH, preferred_element_type=jnp.float32)  92.3 us
    another operation x15, other arithmetic, body(): lower_factor = jnp.linalg.cholesky(symmetric)  79.7 us
    psum x1, waiting for transfers between devices, body(): block = lax.psum(matmul(select_rows, panel_rows), 'scen')  78.9 us
    all_gather x1, waiting for transfers between devices, body(): kkt_all = lax.all_gather(kkt, ('row', 'col'), axis=1, tiled=True)  52.1 us
  transfers between devices with their start and end apart: 17, of which 9 were waited for; matrix products, arithmetic and copies ran while one was open for 19% of the time, Pallas kernels for 0%

profile of v1, /device:TPU:0, one launch (start us, length us, event | category | flops | bytes accessed | tf_op | source)
XLA Modules:
  0.0 1363.0 jit_solution(4824254132349519217)
XLA Ops:
  11.0 52.1 %all-gather.11.cloned.1.call-done = f32[3,768,768]{2,1,0:T(8,128)} async-done(((f32[3,192,768]{2,1,0:T(8,128)}), f32[3,768,768]{2,1,0:T(8,128)}) %all-gather.11.cloned.1.call-update) | async-done | bytes 7077904 | tf_op jit(solution)/shard_map/all_gather | solution.py:34
  63.1 5.7 slice_bitcast_fusion
  68.8 12.0 gather_fusion.1
  80.8 12.5 gather_fusion.2
  93.5 6.3 gather_fusion
  106.1 108.1 %collective-permute-done = f32[3,768,1024]{2,1,0:T(8,128)} collective-permute-done((f32[3,768,1024]{2,1,0:T(8,128)}, f32[3,768,1024]{2,1,0:T(8,128)}, u32[]{:S(2)}, u32[]{:S(2)}) %collective-permute-start) | collective-permute-done | bytes 9437216 | tf_op jit(solution)/shard_map/ppermute | solution.py:16
  214.2 10.3 fusion
  224.6 3.6 copy.12
  228.1 7.4 stack.30
  235.6 6.4 all-to-all-start.1
  242.0 4.5 fusion.16
  246.5 4.5 convolution_subtract_fusion.1
  251.4 4.5 fusion.20
  255.9 4.5 convolution_subtract_fusion.3
  262.8 142.5 %all-to-all-done.1 = f32[4,768,1024]{1,2,0:T(8,128)} async-done(((f32[4,768,1024]{1,2,0:T(8,128)}), f32[4,768,1024]{1,2,0:T(8,128)}, u32[]{:S(2)}, u32[]{:S(2)}) %all-to-all-start.1) | async-done | bytes 12582944 | tf_op jit(solution)/shard_map/all_to_all | solution.py:77
  405.3 7.4 stack.13
  412.7 6.3 all-to-all-start
  419.0 4.5 fusion.24
  423.6 4.5 convolution_subtract_fusion.5
  428.7 4.4 fusion.98
  433.1 4.5 convolution_subtract_fusion
  437.6 4.6 fusion.97
  442.3 4.5 convolution_subtract_fusion.2
  446.8 3.6 copy.13
  450.4 144.6 %all-to-all-done = f32[4,768,1024]{1,2,0:T(8,128)} async-done(((f32[4,768,1024]{1,2,0:T(8,128)}), f32[4,768,1024]{1,2,0:T(8,128)}, u32[]{:S(2)}, u32[]{:S(2)}) %all-to-all-start) | async-done | bytes 12582944 | tf_op jit(solution)/shard_map/all_to_all | solution.py:77
  595.0 7.4 stack.32
  602.4 6.3 all-to-all-start.2
  608.9 4.4 fusion.96
  613.3 4.5 convolution_subtract_fusion.4
  617.9 11.1 fusion.105
  629.0 11.3 fusion.103
  640.2 16.4 %all-gather.17.cloned.1.call-done = f32[768,768]{1,0:T(8,128)} async-done(((f32[192,768]{1,0:T(8,128)}), f32[768,768]{1,0:T(8,128)}) %all-gather.17.cloned.1.call-update) | async-done | bytes 2359312 | tf_op jit(solution)/shard_map/all_gather | solution.py:69
  656.7 9.6 fusion.101
  666.3 44.9 %fusion.104 = f32[4096,1024]{1,0:T(8,128)} fusion(f32[768,4096]{0,1:T(8,128)} %bitcast.10, f32[768,1024]{1,0:T(8,128)S(1)} %copy-done.2), kind=kOutput, calls=%fused_computation.174 | convolution fusion | flops 38654705664 | bytes 32505856 | tf_op jit(solution)/shard_map/dot_general | solution.py:24
  711.3 45.3 %fusion.102 = f32[4096,1024]{1,0:T(8,128)} fusion(f32[768,4096]{0,1:T(8,128)} %bitcast.3, f32[768,1024]{1,0:T(8,128)S(1)} %fusion.101), kind=kOutput, calls=%fused_computation.172 | convolution fusion | flops 38654705664 | bytes 32505856 | tf_op jit(solution)/shard_map/dot_general | solution.py:24
  759.4 47.3 %add_add_fusion = f32[4096,1024]{1,0:T(8,128)} fusion(f32[4096,1024]{1,0:T(8,128)} %fusion.102, f32[4096,1024]{1,0:T(8,128)} %fusion.104, f32[768,4096]{0,1:T(8,128)} %bitcast.17, f32[768,1024]{1,0:T(8,128)S(1)} %copy-done), kind=kOutput, calls=%fused_computation.5 | convolution fusion | flops 38663094272 | bytes 66060288 | tf_op jit(solution)/shard_map/dot_general | solution.py:24
  807.5 280.3 %reduce-scatter.2.cloned.1.call-done = f32[512,1024]{1,0:T(8,128)} async-done(((f32[4096,1024]{1,0:T(8,128)}), f32[512,1024]{1,0:T(8,128)}) %reduce-scatter.2.cloned.1.call-update) | async-done | bytes 2097168 | tf_op jit(solution)/shard_map/reduce_scatter | solution.py:85
  1094.2 35.3 %all-reduce.4.cloned.1.call-done = f32[512,512]{1,0:T(8,128)} async-done(((f32[512,512]{1,0:T(8,128)}), f32[512,512]{1,0:T(8,128)}) %all-reduce.4.cloned.1.call-update) | async-done | bytes 1048592 | tf_op jit(solution)/shard_map/psum | solution.py:95
  1132.9 78.9 %all-reduce.6.cloned.1.call-done = f32[512,512]{0,1:T(8,128)} async-done(((f32[512,512]{0,1:T(8,128)}), f32[512,512]{0,1:T(8,128)}) %all-reduce.6.cloned.1.call-update) | async-done | bytes 1048592 | tf_op jit(solution)/shard_map/psum | solution.py:96
  1215.5 11.7 cholesky.104
  1227.4 9.8 custom-call.30
  1237.8 12.1 cholesky.217
  1251.4 9.8 custom-call.31
  1261.8 11.7 cholesky.238
  1274.3 9.8 custom-call.32
  1284.7 11.9 cholesky.255
  1299.9 10.5 while.1
  1310.5 40.1 %custom-call.33 = f32[4,128,128]{1,2,0:T(8,128)S(1)} custom-call(f32[4,128,128]{2,1,0:T(8,128)} %get-tuple-element.9), custom_call_target="InvertDiagBlocksLowerTriangular" | custom-call | tf_op jit(solution)/shard_map/triangular_solve | solution.py:99
  (112 shorter events, 50.3 us)
Async XLA Ops:
  7.2 56.0 %all-gather.11.cloned.1.call-start = ((), (), s32[]{:S(2)}) async-start(), calls=%async_computation.4 | async-start | bytes 8847360 | tf_op jit(solution)/shard_map/all_gather | solution.py:34
  7.9 238.6 %all-gather.25.cloned.1.call-start = ((), (), s32[]{:S(2)}) async-start(), calls=%async_computation.11 | async-start | bytes 2949120 | tf_op jit(solution)/shard_map/all_gather | solution.py:60
  7.9 206.3 %collective-permute-start = (f32[3,768,1024]{2,1,0:T(8,128)}, f32[3,768,1024]{2,1,0:T(8,128)}, u32[]{:S(2)}, u32[]{:S(2)}) collective-permute-start(f32[3,768,1024]{2,1,0:T(8,128)} %param.6), channel_id=1, source_target_pairs={{0,4},{4,0},{8,12},{12,8},{16,20},{20,16},{24,28},{28,24},{1,5},{5... | collective-permute-start | bytes 28311560 | tf_op jit(solution)/shard_map/ppermute | solution.py:16
  99.8 3.8 copy-start.4
  102.8 153.1 %all-gather.19.cloned.1.call-start = ((), (), s32[]{:S(2)}) async-start(), calls=%async_computation.8 | async-start | bytes 2949120 | tf_op jit(solution)/shard_map/all_gather | solution.py:60
  103.6 320.0 %all-gather.13.cloned.1.call-start = ((), (), s32[]{:S(2)}) async-start(), calls=%async_computation.5 | async-start | bytes 2949120 | tf_op jit(solution)/shard_map/all_gather | solution.py:60
  235.6 169.8 %all-to-all-start.1 = ((f32[4,768,1024]{1,2,0:T(8,128)}), f32[4,768,1024]{1,2,0:T(8,128)}, u32[]{:S(2)}, u32[]{:S(2)}) async-start(f32[4,768,1024]{1,2,0:T(8,128)} %stack.30), calls=%async_computation.1 | async-start | bytes 25165824 | tf_op jit(solution)/shard_map/all_to_all | solution.py:77
  241.9 191.1 %all-gather.27.cloned.1.call-start = ((), (), s32[]{:S(2)}) async-start(), calls=%async_computation.12 | async-start | bytes 2949120 | tf_op jit(solution)/shard_map/all_gather | solution.py:60
  251.1 191.2 %all-gather.21.cloned.1.call-start = ((), (), s32[]{:S(2)}) async-start(), calls=%async_computation.9 | async-start | bytes 2949120 | tf_op jit(solution)/shard_map/all_gather | solution.py:60
  412.7 182.3 %all-to-all-start = ((f32[4,768,1024]{1,2,0:T(8,128)}), f32[4,768,1024]{1,2,0:T(8,128)}, u32[]{:S(2)}, u32[]{:S(2)}) async-start(f32[4,768,1024]{1,2,0:T(8,128)} %stack.13), calls=%async_computation | async-start | bytes 25165824 | tf_op jit(solution)/shard_map/all_to_all | solution.py:77
  419.0 194.3 %all-gather.15.cloned.1.call-start = ((), (), s32[]{:S(2)}) async-start(), calls=%async_computation.6 | async-start | bytes 2949120 | tf_op jit(solution)/shard_map/all_gather | solution.py:60
  428.1 189.8 %all-gather.29.cloned.1.call-start = ((), (), s32[]{:S(2)}) async-start(), calls=%async_computation.13 | async-start | bytes 2949120 | tf_op jit(solution)/shard_map/all_gather | solution.py:69
  437.6 191.4 %all-gather.23.cloned.1.call-start = ((), (), s32[]{:S(2)}) async-start(), calls=%async_computation.10 | async-start | bytes 2949120 | tf_op jit(solution)/shard_map/all_gather | solution.py:69
  602.4 157.1 %all-to-all-start.2 = ((f32[4,768,1024]{1,2,0:T(8,128)}), f32[4,768,1024]{1,2,0:T(8,128)}, u32[]{:S(2)}, u32[]{:S(2)}) async-start(f32[4,768,1024]{1,2,0:T(8,128)} %stack.32), calls=%async_computation.2 | async-start | bytes 25165824 | tf_op jit(solution)/shard_map/all_to_all | solution.py:77
  608.7 48.0 %all-gather.17.cloned.1.call-start = ((), (), s32[]{:S(2)}) async-start(), calls=%async_computation.7 | async-start | bytes 2949120 | tf_op jit(solution)/shard_map/all_gather | solution.py:69
  617.8 469.9 %reduce-scatter.2.cloned.1.call-start = ((), (), s32[]{:S(2)}) async-start(), calls=%async_computation.14 | async-start | bytes 18874368 | tf_op jit(solution)/shard_map/reduce_scatter | solution.py:85
  656.7 9.7 copy-start.2
  711.3 48.1 %copy-start = (f32[768,1024]{1,0:T(8,128)S(1)}, f32[768,1024]{1,0:T(8,128)}, u32[]{:S(2)}) copy-start(f32[768,1024]{1,0:T(8,128)} %fusion.105) | copy-start | bytes 9437188
  806.7 0.7 copy-start.6
  806.7 281.0 %copy-start.5 = (f32[512]{0:T(512)S(1)}, f32[512]{0:T(512)}, u32[]{:S(2)}) copy-start(f32[512]{0:T(512)} %param.7) | copy-start | bytes 6148
  806.8 322.7 %all-reduce.4.cloned.1.call-start = ((), (), s32[]{:S(2)}) async-start(), calls=%async_computation.15 | async-start | bytes 2097152 | tf_op jit(solution)/shard_map/psum | solution.py:95
  1089.6 1.3 copy-start.3
  1094.0 117.9 %all-reduce.6.cloned.1.call-start = ((), (), s32[]{:S(2)}) async-start(), calls=%async_computation.16 | async-start | bytes 2097152 | tf_op jit(solution)/shard_map/psum | solution.py:96
  1237.2 113.4 %copy-start.1 = (f32[512,512]{1,0:T(8,128)S(1)}, f32[512,512]{1,0:T(8,128)}, u32[]{:S(2)}) copy-start(f32[512,512]{1,0:T(8,128)} %all-reduce.4.cloned.1.call-done) | copy-start | bytes 3145732
Sparse Core Ops, SparseCore 0:
  9.5 53.5 all-gather.10
  102.9 24.0 all-gather.24
  128.6 24.0 all-gather.18
  154.1 24.0 all-gather.12
  251.2 38.6 all-gather.26
  291.3 36.8 all-gather.20
  428.2 38.6 all-gather.14
  468.5 36.7 all-gather.28
  506.9 36.7 all-gather.22
  618.0 38.6 all-gather.16
  806.9 280.8 reduce-scatter.1
  1094.1 35.3 all-reduce.3
  1133.0 78.7 all-reduce.5
